TPU v7x, 32 devices: a whole 2x2x4 slice. The times are simulated.
32 devices in a mesh: grp: 4 (over z), seq: 8 (over y, x, core).
Axes of the slice: x: 2, y: 2, z: 4, core: 2. Of those that a mesh axis runs over, the one named last changes fastest.
Arguments:
- fine_rows: bfloat16 [4, 1024, 2048], P('grp', 'seq'), may hold values from -6 to 6
- segment_ids: int32 [4, 1024], P('grp', 'seq'), may hold values from 0 to 7, as said below
- pool_gain: float32 [2048], replicated, may hold values from 0.1 to 1.9
- w_in: bfloat16 [2048, 8192], P('grp', 'seq'), may hold values from -0.125 to 0.125
- w_gate: bfloat16 [8192, 16384], P('grp', 'seq'), may hold values from -0.0625 to 0.0625
- w_up: bfloat16 [8192, 16384], P('grp', 'seq'), may hold values from -0.0625 to 0.0625
- w_down: bfloat16 [16384, 8192], P('seq', 'grp'), may hold values from -0.046875 to 0.046875
- out_grad: bfloat16 [4, 64, 8192], P('grp'), may hold values from -6 to 6
Outputs:
- coarse_out: bfloat16 [4, 64, 8192], P('grp', None, 'seq')
- fine_grad: bfloat16 [4, 1024, 2048], P('grp', 'seq')
Inputs may be any that keep to these rules, and one draw needn't show every extreme that they name: `segment_ids`: within each shard of 128 consecutive bytes the numbers count the shard's segments from 0 upward, never falling, every segment one byte or more; a shard holds 4 to 8 segments, some shard of every document exactly 8, and every document 48 segments in all.
All inputs are finite; a program needn't handle non-finite values.
Results may differ from a plain program's by a relative error of at most 0.02.
Values may be sent and summed in bfloat16 or wider, within the bound.
A program may use at most 192 MiB of HBM per device.

v0:
```python
import jax
import jax.numpy as jnp
from jax import lax
from jax.sharding import PartitionSpec as P

SEG_CAP = 8


norm_eps = 1e-06


def silu_parts(gate_value):
    sigma = jax.nn.sigmoid(gate_value)
    return (gate_value * sigma, sigma * (1.0 + gate_value * (1.0 - sigma)))


def column_total(partial_value):
    return lax.psum_scatter(
        partial_value.astype(jnp.bfloat16), "seq", scatter_dimension=1, tiled=True
    ).astype(jnp.float32)


def shards(fine_rows, segment_ids, pool_gain, w_in, w_gate, w_up, w_down, out_grad):
    rows_here = fine_rows[0]
    index_here = segment_ids[0]
    slots = jnp.arange(SEG_CAP, dtype=jnp.int32)
    member = index_here[None, :] == slots[:, None]
    segment_sums = jnp.dot(
        member.astype(jnp.bfloat16), rows_here, preferred_element_type=jnp.float32
    )
    inv_rms = lax.rsqrt(jnp.mean(segment_sums * segment_sums, axis=1, keepdims=True) + norm_eps)
    pooled = (segment_sums * inv_rms * pool_gain).astype(jnp.bfloat16)
    full_in, full_gate, full_up, full_down = (
        lax.all_gather(w_in, "grp", axis=0, tiled=True),
        lax.all_gather(w_gate, "grp", axis=0, tiled=True),
        lax.all_gather(w_up, "grp", axis=0, tiled=True),
        lax.all_gather(w_down, "grp", axis=1, tiled=True),
    )
    grad_rows = out_grad[0]
    live_count = (jnp.max(index_here) + 1).astype(jnp.bfloat16).reshape(1)
    gathered, all_counts = (
        lax.all_gather(pooled, "seq", axis=0, tiled=True),
        lax.all_gather(live_count, "seq", axis=0, tiled=True),
    )
    shard_counts = all_counts.astype(jnp.int32)
    offsets = jnp.cumsum(shard_counts) - shard_counts
    slot_index = jnp.arange(gathered.shape[0], dtype=jnp.int32)
    shard_of = slot_index // SEG_CAP
    within = slot_index % SEG_CAP
    shard_match = shard_of[:, None] == jnp.arange(shard_counts.shape[0], dtype=jnp.int32)[None, :]
    start_of = jnp.sum(jnp.where(shard_match, offsets[None, :], 0), axis=1)
    count_of = jnp.sum(jnp.where(shard_match, shard_counts[None, :], 0), axis=1)
    target = start_of + within
    is_live = within < count_of
    live_rows = gathered.shape[0] * 3 // 4
    select = (target[None, :] == jnp.arange(live_rows, dtype=jnp.int32)[:, None]) & is_live[None, :]
    selector = select.astype(jnp.bfloat16)
    work_in = jnp.dot(selector, gathered, preferred_element_type=jnp.float32).astype(jnp.bfloat16)
    work_grad = jnp.dot(selector, grad_rows, preferred_element_type=jnp.float32).astype(
        jnp.bfloat16
    )
    col_width = full_in.shape[1]
    x_cols = jnp.dot(work_in, full_in, preferred_element_type=jnp.float32).astype(jnp.bfloat16)
    coarse_x = lax.all_gather(x_cols, "seq", axis=1, tiled=True)
    gate_value = jnp.dot(coarse_x, full_gate, preferred_element_type=jnp.float32)
    up_value = jnp.dot(coarse_x, full_up, preferred_element_type=jnp.float32)
    activated, derivative = silu_parts(gate_value)
    hidden = (activated * up_value).astype(jnp.bfloat16)
    down_cols = column_total(jnp.dot(hidden, full_down, preferred_element_type=jnp.float32))
    out_cols = (x_cols.astype(jnp.float32) + down_cols).astype(jnp.bfloat16)
    grad_hidden = jnp.dot(work_grad, full_down.T, preferred_element_type=jnp.float32)
    grad_gate = (grad_hidden * up_value * derivative).astype(jnp.bfloat16)
    grad_up = (grad_hidden * activated).astype(jnp.bfloat16)
    back_part = jnp.dot(grad_gate, full_gate.T, preferred_element_type=jnp.float32)
    back_part = back_part + jnp.dot(grad_up, full_up.T, preferred_element_type=jnp.float32)
    back_cols = column_total(back_part)
    col_start = lax.axis_index("seq") * col_width
    grad_cols = lax.dynamic_slice_in_dim(work_grad, col_start, col_width, 1)
    grad_x = (back_cols + grad_cols.astype(jnp.float32)).astype(jnp.bfloat16)
    term = jnp.dot(grad_x, full_in.T, preferred_element_type=jnp.float32)
    term = jnp.dot(select.astype(jnp.float32).T, term, precision=lax.Precision.HIGHEST)
    out_cols = jnp.dot(selector.T, out_cols, preferred_element_type=jnp.float32).astype(
        jnp.bfloat16
    )
    grad_pooled = lax.psum_scatter(
        term.astype(jnp.bfloat16), "seq", scatter_dimension=0, tiled=True
    ).astype(jnp.float32)
    weighted = grad_pooled * pool_gain
    inner = jnp.mean(weighted * segment_sums, axis=1, keepdims=True)
    grad_sums = inv_rms * weighted - segment_sums * (inv_rms * inv_rms * inv_rms) * inner
    fine_grad = jnp.dot(member.astype(jnp.float32).T, grad_sums, precision=lax.Precision.HIGHEST)
    return (out_cols[None], fine_grad.astype(jnp.bfloat16)[None])


def solution(mesh):
    return jax.shard_map(
        shards,
        mesh=mesh,
        in_specs=(
            P("grp", "seq", None),
            P("grp", "seq"),
            P(),
            P("grp", "seq"),
            P("grp", "seq"),
            P("grp", "seq"),
            P("seq", "grp"),
            P("grp", None, None),
        ),
        out_specs=(P("grp", None, "seq"), P("grp", "seq", None)),
        check_vma=False,
    )
```

profile of v0, /device:TPU:2, one launch (start us, length us, event | category | flops | bytes accessed | tf_op | source)
XLA Modules:
  0.0 1940.5 jit_solution(14127923532419282116)
XLA Ops:
  7.2 0.7 all-gather.5.cloned.1.call-update
  8.0 0.7 all-gather.9.cloned.1.call-update
  8.7 0.7 all-gather.7.cloned.1.call-update
  9.4 0.5 all-gather.11.cloned.1.call-update
  10.0 1.3 reduce_max.9
  12.0 1.2 dynamic-slice
  13.2 0.8 dynamic-update-slice
  14.0 11.0 all-reduce
  25.2 1.4 multiply_reduce_fusion.1
  26.6 0.8 multiply_convert_fusion.6
  27.4 11.3 all_gather.22
  38.9 0.3 convolution_convert_fusion.1
  39.2 52.4 %all-gather.5.cloned.1.call-done = bf16[2048,1024]{1,0:T(8,128)(2,1)} async-done(((bf16[512,1024]{1,0:T(8,128)(2,1)}), bf16[2048,1024]{1,0:T(8,128)(2,1)}) %all-gather.5.cloned.1.call-update) | async-done | bytes 4194320 | tf_op jit(solution)/shard_map/all_gather | solution.py:34
  91.6 3.1 fusion.3
  94.8 10.5 all_gather.24
  105.3 547.8 %all-gather.9.cloned.1.call-done = bf16[8192,2048]{1,0:T(8,128)(2,1)} async-done(((bf16[2048,2048]{1,0:T(8,128)(2,1)}), bf16[8192,2048]{1,0:T(8,128)(2,1)}) %all-gather.9.cloned.1.call-update) | async-done | bytes 33554448 | tf_op jit(solution)/shard_map/all_gather | solution.py:36
  653.1 17.3 fusion.48
  670.5 543.9 %all-gather.7.cloned.1.call-done = bf16[8192,2048]{1,0:T(8,128)(2,1)} async-done(((bf16[2048,2048]{1,0:T(8,128)(2,1)}), bf16[8192,2048]{1,0:T(8,128)(2,1)}) %all-gather.7.cloned.1.call-update) | async-done | bytes 33554448 | tf_op jit(solution)/shard_map/all_gather | solution.py:35
  1214.3 17.5 fusion.47
  1231.8 543.6 %all-gather.11.cloned.1.call-done = bf16[2048,8192]{1,0:T(8,128)(2,1)} async-done(((bf16[2048,2048]{1,0:T(8,128)(2,1)}), bf16[2048,8192]{1,0:T(8,128)(2,1)}) %all-gather.11.cloned.1.call-update) | async-done | bytes 33554448 | tf_op jit(solution)/shard_map/all_gather | solution.py:37
  1775.4 15.2 fusion.49
  1790.6 15.5 fusion.9
  1806.1 15.8 fusion
  1822.3 15.0 convolution_convert_fusion
  1837.3 18.0 reduce-scatter.6.cloned.1.call-done
  1855.3 3.6 fusion.11
  1858.9 1.1 convolution_convert_fusion.3
  1860.1 33.2 %reduce-scatter.4.cloned.1.call-done = bf16[48,1024]{1,0:T(8,128)(2,1)} async-done(((bf16[48,8192]{1,0:T(8,128)(2,1)}), bf16[48,1024]{1,0:T(8,128)(2,1)}) %reduce-scatter.4.cloned.1.call-update) | async-done | bytes 98320 | tf_op jit(solution)/shard_map/reduce_scatter | solution.py:18
  1893.3 1.8 fusion.4
  1895.1 35.5 %reduce-scatter.8.cloned.1.call-done = bf16[8,2048]{1,0:T(8,128)(2,1)} async-done(((bf16[64,2048]{1,0:T(8,128)(2,1)}), bf16[8,2048]{1,0:T(8,128)(2,1)}) %reduce-scatter.8.cloned.1.call-update) | async-done | bytes 32784 | tf_op jit(solution)/shard_map/reduce_scatter | solution.py:85
  1930.6 0.9 multiply_reduce_fusion
  1931.5 2.2 fusion.1
  (28 shorter events, 0.9 us)
Async XLA Ops:
  7.2 31.7 %copy-start = (bf16[1,64,8192]{2,1,0:T(8,128)(2,1)S(1)}, bf16[1,64,8192]{2,1,0:T(8,128)(2,1)}, u32[]{:S(2)}) copy-start(bf16[1,64,8192]{2,1,0:T(8,128)(2,1)} %param.15) | copy-start | bytes 3145732
  7.2 84.5 %all-gather.5.cloned.1.call-start = ((), (), s32[]{:S(2)}) async-start(), calls=%async_computation.3 | async-start | bytes 5242880 | tf_op jit(solution)/shard_map/all_gather | solution.py:34
  7.9 645.2 %all-gather.9.cloned.1.call-start = ((), (), s32[]{:S(2)}) async-start(), calls=%async_computation.5 | async-start | bytes 41943040 | tf_op jit(solution)/shard_map/all_gather | solution.py:36
  8.7 1205.7 %all-gather.7.cloned.1.call-start = ((), (), s32[]{:S(2)}) async-start(), calls=%async_computation.4 | async-start | bytes 41943040 | tf_op jit(solution)/shard_map/all_gather | solution.py:35
  9.4 1766.0 %all-gather.11.cloned.1.call-start = ((), (), s32[]{:S(2)}) async-start(), calls=%async_computation.6 | async-start | bytes 41943040 | tf_op jit(solution)/shard_map/all_gather | solution.py:37
  10.0 1845.3 %reduce-scatter.6.cloned.1.call-start = ((), (), s32[]{:S(2)}) async-start(), calls=%async_computation.8 | async-start | bytes 884736 | tf_op jit(solution)/shard_map/reduce_scatter | solution.py:18
  1806.1 127.6 %copy-start.1 = (bf16[1,64,8192]{2,1,0:T(8,128)(2,1)S(1)}, bf16[1,64,8192]{2,1,0:T(8,128)(2,1)}, u32[]{:S(2)}) copy-start(bf16[1,64,8192]{2,1,0:T(8,128)(2,1)} %param.15) | copy-start | bytes 3145732
  1822.0 108.6 %copy-start.2 = (f32[2048]{0:T(1024)S(1)}, f32[2048]{0:T(1024)}, u32[]{:S(2)}) copy-start(f32[2048]{0:T(1024)} %param.10) | copy-start | bytes 24580
  1822.0 109.5 %copy-start.3 = (s32[1,128]{1,0:T(1,128)S(1)}, s32[1,128]{1,0:T(1,128)}, u32[]{:S(2)}) copy-start(s32[1,128]{1,0:T(1,128)} %param.9) | copy-start | bytes 1540
  1822.0 71.4 %reduce-scatter.4.cloned.1.call-start = ((), (), s32[]{:S(2)}) async-start(), calls=%async_computation.7 | async-start | bytes 884736 | tf_op jit(solution)/shard_map/reduce_scatter | solution.py:18
  1837.3 93.3 %reduce-scatter.8.cloned.1.call-start = ((), (), s32[]{:S(2)}) async-start(), calls=%async_computation.9 | async-start | bytes 294912 | tf_op jit(solution)/shard_map/reduce_scatter | solution.py:85
Sparse Core Ops, SparseCore 0:
  9.6 82.0 all-gather.4
  93.2 559.8 all-gather.8
  654.7 559.5 all-gather.6
  1215.8 559.5 all-gather.10
  1822.1 33.1 reduce-scatter.5
  1858.3 34.9 reduce-scatter.3
  1896.9 33.6 reduce-scatter.7
where the time goes:
time: 1940 us
  waiting for transfers between devices  1780 us (92%)
  matrix products  110 us (6%)
  blocking collectives  32.9 us (2%)
    all_gather x1, waiting for transfers between devices, shards(): lax.all_gather(w_up, 'grp', axis=0, tiled=True)  548 us
    all_gather x1, waiting for transfers between devices, shards(): lax.all_gather(w_gate, 'grp', axis=0, tiled=True)  544 us
    all_gather x1, waiting for transfers between devices, shards(): lax.all_gather(w_down, 'grp', axis=1, tiled=True)  544 us
    all_gather x1, waiting for transfers between devices, shards(): lax.all_gather(w_in, 'grp', axis=0, tiled=True)  52.4 us
    reduce_scatter x2, waiting for transfers between devices, column_total(): lax.psum_scatter(partial_value.astype(jnp.bfloat16), 'seq', scatter_dimen...  51.3 us
  transfers between devices with their start and end apart: 7, of which 7 were waited for; matrix products, arithmetic and copies ran while one was open for 3% of the time, Pallas kernels for 0%

commit v1 on v0

v1 whole, which is shorter than its diff:
```python
import jax
import jax.numpy as jnp
from jax import lax
from jax.sharding import PartitionSpec as P

SEG_CAP = 8


norm_eps = 1e-06
bf16 = jnp.bfloat16
f32 = jnp.float32


def silu_parts(gate_value):
    sigma = jax.nn.sigmoid(gate_value)
    return (gate_value * sigma, sigma * (1.0 + gate_value * (1.0 - sigma)))


def matmul(a, b):
    return jnp.dot(a, b, preferred_element_type=f32)


def matmul_t(a, b):
    return lax.dot_general(a, b, (((1,), (1,)), ((), ())), preferred_element_type=f32)


def swap_pairs(grps, seqs):
    halves = seqs // grps
    return [
        (g * seqs + p * halves + h, p * seqs + g * halves + h)
        for g in range(grps)
        for p in range(grps)
        for h in range(halves)
    ]


def grp_total(partial_value):
    return lax.psum_scatter(
        partial_value.astype(bf16), "grp", scatter_dimension=0, tiled=True
    ).astype(f32)


def make_shards(grps, seqs):
    halves = seqs // grps
    pairs = swap_pairs(grps, seqs)

    def swap(value):
        return lax.ppermute(value, ("grp", "seq"), pairs)

    def shards(fine_rows, segment_ids, pool_gain, w_in, w_gate, w_up, w_down, out_grad):
        rows_here = fine_rows[0]
        index_here = segment_ids[0]
        feat, width = w_in.shape
        slots = jnp.arange(SEG_CAP, dtype=jnp.int32)
        member = index_here[None, :] == slots[:, None]
        segment_sums = matmul(member.astype(bf16), rows_here)
        inv_rms = lax.rsqrt(jnp.mean(segment_sums * segment_sums, axis=1, keepdims=True) + norm_eps)
        pooled = (segment_sums * inv_rms * pool_gain).astype(bf16)
        live_count = jnp.max(index_here) + 1
        packed = jnp.concatenate(
            [pooled, jnp.full((1, pooled.shape[1]), live_count.astype(bf16))], axis=0
        )
        gathered = lax.all_gather(packed, "seq", axis=0)
        shard_counts = gathered[:, SEG_CAP, 0].astype(jnp.int32)
        gathered = gathered[:, :SEG_CAP].reshape(seqs * SEG_CAP, -1)
        offsets = jnp.cumsum(shard_counts) - shard_counts
        slot_count = seqs * SEG_CAP
        within = jnp.tile(slots, seqs)
        target = jnp.repeat(offsets, SEG_CAP) + within
        is_live = within < jnp.repeat(shard_counts, SEG_CAP)
        rows = slot_count * 3 // 4
        select = (target[None, :] == jnp.arange(rows, dtype=jnp.int32)[:, None]) & is_live[None, :]
        selector = select.astype(bf16)
        work_in = matmul(selector, gathered).astype(bf16)
        work_in = lax.all_to_all(
            work_in.reshape(rows, grps, feat), "grp", split_axis=1, concat_axis=0
        ).reshape(grps * rows, feat)
        x_cols = grp_total(matmul(work_in, w_in)).astype(bf16)

        seq_at = lax.axis_index("seq")
        block = w_gate.shape[0]
        piece = block // seqs
        grad_here = out_grad[0].reshape(slot_count, grps, seqs, piece)
        grad_part = lax.dynamic_index_in_dim(grad_here, seq_at, 2, keepdims=False)
        grad_part = matmul(selector, grad_part.reshape(slot_count, grps * piece)).astype(bf16)
        grad_part = lax.all_to_all(
            grad_part.reshape(rows, grps, piece), "grp", split_axis=1, concat_axis=0
        ).reshape(grps * rows, piece)
        work_grad = lax.all_gather(grad_part, "seq", axis=1, tiled=True)
        grad_hidden = grp_total(matmul_t(work_grad, w_down))

        def spread(cols):
            every = lax.all_gather(swap(cols), "seq", axis=0)
            every = every.reshape(grps, halves, rows, width)
            return every.transpose(0, 2, 1, 3).reshape(grps * rows, halves * width)

        def column_total(part):
            part = part.astype(bf16).reshape(grps, rows, halves, width)
            part = part.transpose(0, 2, 1, 3).reshape(seqs * rows, width)
            return swap(lax.psum_scatter(part, "seq", scatter_dimension=0, tiled=True)).astype(f32)

        coarse_x = spread(x_cols)
        gate_value = grp_total(matmul(coarse_x, w_gate))
        up_value = grp_total(matmul(coarse_x, w_up))
        activated, derivative = silu_parts(gate_value)
        hidden = (activated * up_value).astype(bf16)
        grad_gate = (grad_hidden * up_value * derivative).astype(bf16)
        grad_up = (grad_hidden * activated).astype(bf16)
        grad_gate = lax.all_gather(grad_gate, "grp", axis=0, tiled=True)
        grad_up = lax.all_gather(grad_up, "grp", axis=0, tiled=True)
        hidden = lax.all_gather(hidden, "grp", axis=0, tiled=True)
        back_cols = column_total(matmul_t(grad_gate, w_gate) + matmul_t(grad_up, w_up))
        down_cols = column_total(matmul(hidden, w_down))
        out_cols = (x_cols.astype(f32) + down_cols).astype(bf16)
        out_cols = matmul(selector.T, out_cols).astype(bf16)

        grad_cols = lax.dynamic_slice_in_dim(out_grad[0], seq_at * width, width, 1)
        grad_cols = matmul(selector, grad_cols)
        grad_x = (back_cols + grad_cols).astype(bf16)
        grad_x = lax.all_gather(grad_x, "grp", axis=0, tiled=True)
        term = matmul_t(grad_x, w_in).astype(bf16)
        term = lax.all_to_all(
            term.reshape(grps, rows, feat), "grp", split_axis=0, concat_axis=1
        ).reshape(rows, grps * feat)
        term = matmul(selector.T, term).astype(bf16)
        grad_pooled = lax.psum_scatter(term, "seq", scatter_dimension=0, tiled=True).astype(f32)
        weighted = grad_pooled * pool_gain
        inner = jnp.mean(weighted * segment_sums, axis=1, keepdims=True)
        grad_sums = inv_rms * weighted - segment_sums * (inv_rms * inv_rms * inv_rms) * inner
        fine_grad = matmul(member.astype(bf16).T, grad_sums.astype(bf16)).astype(bf16)
        return (out_cols[None], fine_grad[None])

    return shards


def solution(mesh):
    return jax.shard_map(
        make_shards(mesh.shape["grp"], mesh.shape["seq"]),
        mesh=mesh,
        in_specs=(
            P("grp", "seq", None),
            P("grp", "seq"),
            P(),
            P("grp", "seq"),
            P("grp", "seq"),
            P("grp", "seq"),
            P("seq", "grp"),
            P("grp", None, None),
        ),
        out_specs=(P("grp", None, "seq"), P("grp", "seq", None)),
        check_vma=False,
    )
```

time: 1940 us -> 327 us (0.17)
  waiting for transfers between devices: 1780 us -> 123 us
  blocking collectives: 32.9 us -> 109 us
  matrix products: 110 us -> 45.5 us
    all_gather x4 -> x0, waiting for transfers between devices: 1690 us -> none  [the longest x1 548 us: shards(): lax.all_gather(w_up, 'grp', axis=0, tiled=True)]
    all_gather x2 -> x7, blocking collectives: 21.9 us -> 99.2 us  [the longest x1 18.2 us: shards(): grad_gate = lax.all_gather(grad_gate, 'grp', axis=0, tiled=True)]
    dot_general x13 -> x15, matrix products: 110 us -> 45.5 us  [the longest x11 25.1 us: matmul(): return jnp.dot(a, b, preferred_element_type=f32)]
    ppermute x0 -> x3, waiting for transfers between devices: none -> 24.4 us  [swap(): return lax.ppermute(value, ('grp', 'seq'), pairs)]
    reduce_scatter x3 -> x7, waiting for transfers between devices: 86.7 us -> 89.3 us  [the longest x4 40.2 us: grp_total(): lax.psum_scatter(partial_value.astype(bf16), 'grp', scatter_dimension=0,...]
  transfers between devices with their start and end apart: 7 -> 12, of which waited for: 7 -> 10; matrix products, arithmetic and copies ran while one was open for 3% -> 11% of each run, Pallas kernels for 0% -> 0%
where the time goes in v1:
time: 327 us; the launch traced here: 324 us
  waiting for transfers between devices  123 us (38%)
  blocking collectives  109 us (33%)
  matrix products  45.5 us (14%)
  starting transfers between devices  18.1 us (6%)
  between operations  15 us (5%)
  local copies, waits for them, and re-layouts  8.57 us (3%)
  other arithmetic  4.91 us (2%)
    reduce_scatter x4, waiting for transfers between devices, grp_total(): lax.psum_scatter(partial_value.astype(bf16), 'grp', scatter_dimension=0,...  40.2 us
    reduce_scatter x1, waiting for transfers between devices, shards(): lax.psum_scatter(term, 'seq', scatter_dimension=0, tiled=True).astype(f32)  25.1 us
    dot_general x11, matrix products, matmul(): return jnp.dot(a, b, preferred_element_type=f32)  25.1 us
    ppermute x3, waiting for transfers between devices, swap(): return lax.ppermute(value, ('grp', 'seq'), pairs)  24.4 us
    reduce_scatter x2, waiting for transfers between devices, column_total(): lax.psum_scatter(part, 'seq', scatter_dimension=0, tiled=True)  24 us
    dot_general x4, matrix products, matmul_t(): lax.dot_general(a, b, (((1,), (1,)), ((), ())), preferred_element_type=f32)  20.3 us
    all_gather x1, blocking collectives, shards(): grad_gate = lax.all_gather(grad_gate, 'grp', axis=0, tiled=True)  18.2 us
    all_gather x1, blocking collectives, shards(): grad_up = lax.all_gather(grad_up, 'grp', axis=0, tiled=True)  17.4 us
  transfers between devices with their start and end apart: 12, of which 10 were waited for; matrix products, arithmetic and copies ran while one was open for 11% of the time, Pallas kernels for 0%

profile of v1, /device:TPU:2, one launch (start us, length us, event | category | flops | bytes accessed | tf_op | source)
XLA Modules:
  0.0 324.5 jit_solution(11023302746642176019)
XLA Ops:
  7.2 1.4 multiply_reduce_fusion.1
  11.4 9.9 %all-gather.2 = bf16[8,9,2048]{2,1,0:T(8,128)(2,1)S(1)} all-gather(bf16[1,9,2048]{2,1,0:T(8,128)(2,1)S(1)} %pad_bitcast_fusion), channel_id=2, replica_groups=mesh['grp'=4,'seq'=8] {'seq'}, dimensions={0}, use_global_device_ids=true | all-gather | bytes 331776 | tf_op jit(solution)/shard_map/all_gather | solution.py:63
  23.1 4.9 %all-to-all-start = ((bf16[1,48,4,512]{3,1,0,2:T(8,128)(2,1)}), bf16[1,48,4,512]{3,1,0,2:T(8,128)(2,1)S(1)}, u32[]{:S(2)}, u32[]{:S(2)}) async-start(bf16[1,48,4,512]{3,1,0,2:T(8,128)(2,1)} %copy.18), calls=%async_computation | async-start | bytes 393216 | tf_op jit(solution)/shard_map/all_to_all | solution.py:75
  27.9 1.5 copy.28
  31.1 4.8 %all-to-all-done = bf16[1,48,4,512]{3,1,0,2:T(8,128)(2,1)S(1)} async-done(((bf16[1,48,4,512]{3,1,0,2:T(8,128)(2,1)}), bf16[1,48,4,512]{3,1,0,2:T(8,128)(2,1)S(1)}, u32[]{:S(2)}, u32[]{:S(2)}) %all-to-all-start) | async-done | bytes 196640 | tf_op jit(solution)/shard_map/all_to_all | solution.py:75
  35.9 3.3 %all-to-all-start.1 = ((bf16[1,48,4,256]{3,1,0,2:T(8,128)(2,1)}), bf16[1,48,4,256]{3,1,0,2:T(8,128)(2,1)S(1)}, u32[]{:S(2)}, u32[]{:S(2)}) async-start(bf16[1,48,4,256]{3,1,0,2:T(8,128)(2,1)} %copy.22), calls=%async_computation.5 | async-start | bytes 196608 | tf_op jit(solution)/shard_map/all_to_all | solution.py:86
  40.5 4.5 %all-to-all-done.1 = bf16[1,48,4,256]{3,1,0,2:T(8,128)(2,1)S(1)} async-done(((bf16[1,48,4,256]{3,1,0,2:T(8,128)(2,1)}), bf16[1,48,4,256]{3,1,0,2:T(8,128)(2,1)S(1)}, u32[]{:S(2)}, u32[]{:S(2)}) %all-to-all-start.1) | async-done | bytes 98336 | tf_op jit(solution)/shard_map/all_to_all | solution.py:86
  45.0 12.1 %all_gather.32 = bf16[192,2048]{1,0:T(8,128)(2,1)S(1)} all-gather(bf16[192,256]{1,0:T(8,128)(2,1)S(1)} %bitcast.93), channel_id=1, replica_groups=mesh['grp'=4,'seq'=8] {'seq'}, dimensions={1}, use_global_device_ids=true | all-gather | bytes 884736 | tf_op jit(solution)/shard_map/all_gather | solution.py:89
  57.2 7.2 %convolution_convert_fusion = bf16[192,2048]{1,0:T(8,128)(2,1)} fusion(bf16[192,2048]{1,0:T(8,128)(2,1)S(1)} %all_gather.32, bf16[2048,2048]{1,0:T(8,128)(2,1)} %param.14), kind=kOutput, calls=%fused_computation.1 | convolution fusion | flops 1611005952 | bytes 9961472 | tf_op jit(solution)/shard_map/dot_general | solution.py:24
  64.5 2.8 collective-permute-start
  67.3 15.3 %collective-permute-done = bf16[48,1024]{1,0:T(8,128)(2,1)S(1)} collective-permute-done((bf16[48,1024]{1,0:T(8,128)(2,1)}, bf16[48,1024]{1,0:T(8,128)(2,1)S(1)}, u32[]{:S(2)}, u32[]{:S(2)}) %collective-permute-start) | collective-permute-done | bytes 98336 | tf_op jit(solution)/shard_map/ppermute | solution.py:48
  82.6 9.6 %all-gather.1 = bf16[384,1024]{1,0:T(8,128)(2,1)S(1)} all-gather(bf16[48,1024]{1,0:T(8,128)(2,1)S(1)} %collective-permute-done), channel_id=3, replica_groups=mesh['grp'=4,'seq'=8] {'seq'}, dimensions={0}, use_global_device_ids=true | all-gather | bytes 884736 | tf_op jit(solution)/shard_map/all_gather | solution.py:93
  93.2 6.1 %convolution_convert_fusion.3 = bf16[192,2048]{1,0:T(8,128)(2,1)} fusion(bf16[192,2048]{1,0:T(8,128)(2,1)S(1)} %bitcast.87, bf16[2048,2048]{1,0:T(8,128)(2,1)} %param.12), kind=kOutput, calls=%fused_computation.4 | convolution fusion | flops 1611005952 | bytes 9961472 | tf_op jit(solution)/shard_map/dot_general | solution.py:20
  99.4 6.1 %convolution_convert_fusion.2 = bf16[192,2048]{1,0:T(8,128)(2,1)} fusion(bf16[192,2048]{1,0:T(8,128)(2,1)S(1)} %bitcast.88, bf16[2048,2048]{1,0:T(8,128)(2,1)} %param.13), kind=kOutput, calls=%fused_computation.3 | convolution fusion | flops 1611005952 | bytes 9961472 | tf_op jit(solution)/shard_map/dot_general | solution.py:20
  105.5 15.3 %reduce-scatter.10.cloned.1.call-done = bf16[48,2048]{1,0:T(8,128)(2,1)} async-done(((bf16[192,2048]{1,0:T(8,128)(2,1)}), bf16[48,2048]{1,0:T(8,128)(2,1)}) %reduce-scatter.10.cloned.1.call-update) | async-done | bytes 196624 | tf_op jit(solution)/shard_map/reduce_scatter | solution.py:38
  120.8 24.9 %reduce-scatter.12.cloned.1.call-done = bf16[48,2048]{1,0:T(8,128)(2,1)} async-done(((bf16[192,2048]{1,0:T(8,128)(2,1)}), bf16[48,2048]{1,0:T(8,128)(2,1)}) %reduce-scatter.12.cloned.1.call-update) | async-done | bytes 196624 | tf_op jit(solution)/shard_map/reduce_scatter | solution.py:38
  145.7 1.4 fusion.8
  147.1 18.2 %all_gather.33 = bf16[192,2048]{1,0:T(8,128)(2,1)S(1)} all-gather(bf16[48,2048]{1,0:T(8,128)(2,1)S(1)} %get-tuple-element.3), channel_id=1, replica_groups=mesh['grp'=4,'seq'=8] {'grp'}, dimensions={0}, use_global_device_ids=true | all-gather | bytes 983040 | tf_op jit(solution)/shard_map/all_gather | solution.py:109
  165.2 6.3 %fusion.43 = f32[192,2048]{1,0:T(8,128)S(1)} fusion(bf16[192,2048]{1,0:T(8,128)(2,1)S(1)} %all_gather.33, bf16[2048,2048]{1,0:T(8,128)(2,1)} %param.12), kind=kOutput, calls=%fused_computation.73 | convolution fusion | flops 1610612736 | bytes 10747904 | tf_op jit(solution)/shard_map/dot_general | solution.py:24
  171.6 17.4 %all_gather.34 = bf16[192,2048]{1,0:T(8,128)(2,1)S(1)} all-gather(bf16[48,2048]{1,0:T(8,128)(2,1)S(1)} %get-tuple-element.2), channel_id=1, replica_groups=mesh['grp'=4,'seq'=8] {'grp'}, dimensions={0}, use_global_device_ids=true | all-gather | bytes 983040 | tf_op jit(solution)/shard_map/all_gather | solution.py:110
  188.9 6.3 %fusion = bf16[192,2048]{1,0:T(8,128)(2,1)S(1)} fusion(f32[192,2048]{1,0:T(8,128)S(1)} %fusion.43, bf16[192,2048]{1,0:T(8,128)(2,1)S(1)} %all_gather.34, bf16[2048,2048]{1,0:T(8,128)(2,1)} %param.13), kind=kOutput, calls=%fused_computation.5 | convolution fusion | flops 1611399168 | bytes 11534336 | tf_op jit(solution)/shard_map/dot_general | solution.py:24
  196.9 16.8 %all_gather.31 = bf16[192,2048]{1,0:T(8,128)(2,1)S(1)} all-gather(bf16[48,2048]{1,0:T(8,128)(2,1)S(1)} %get-tuple-element.4), channel_id=1, replica_groups=mesh['grp'=4,'seq'=8] {'grp'}, dimensions={0}, use_global_device_ids=true | all-gather | bytes 983040 | tf_op jit(solution)/shard_map/all_gather | solution.py:111
  213.7 18.1 %reduce-scatter.18.cloned.1.call-done = bf16[48,1024]{1,0:T(8,128)(2,1)} async-done(((bf16[384,1024]{1,0:T(8,128)(2,1)}), bf16[48,1024]{1,0:T(8,128)(2,1)}) %reduce-scatter.18.cloned.1.call-update) | async-done | bytes 98320 | tf_op jit(solution)/shard_map/reduce_scatter | solution.py:100
  231.9 3.4 %collective-permute-start.2 = (bf16[48,1024]{1,0:T(8,128)(2,1)}, bf16[48,1024]{1,0:T(8,128)(2,1)S(1)}, u32[]{:S(2)}, u32[]{:S(2)}) collective-permute-start(bf16[48,1024]{1,0:T(8,128)(2,1)} %reduce-scatter.18.cloned.1.call-done), channel_id=1, source_target_pairs={{0,0},{1,1},{2,8},{3,9},{4,16},{5,17},{6,24},{7,25},{8,2},{9,3},{1... | collective-permute-start | bytes 294920 | tf_op jit(solution)/shard_map/ppermute | solution.py:48
  235.3 5.2 %convolution_convert_fusion.1 = bf16[192,2048]{1,0:T(8,128)(2,1)S(1)} fusion(bf16[192,2048]{1,0:T(8,128)(2,1)S(1)} %all_gather.31, bf16[2048,2048]{1,0:T(8,128)(2,1)} %param.14), kind=kOutput, calls=%fused_computation.2 | convolution fusion | flops 1611005952 | bytes 9961472 | tf_op jit(solution)/shard_map/dot_general | solution.py:20
  244.4 15.3 %all_gather.35 = bf16[192,1024]{1,0:T(8,128)(2,1)S(1)} all-gather(bf16[48,1024]{1,0:T(8,128)(2,1)S(1)} %add_convert_fusion), channel_id=1, replica_groups=mesh['grp'=4,'seq'=8] {'grp'}, dimensions={0}, use_global_device_ids=true | all-gather | bytes 491520 | tf_op jit(solution)/shard_map/all_gather | solution.py:120
  260.2 10.1 %all_to_all.45 = bf16[4,48,1,512]{3,1,2,0:T(8,128)(2,1)S(1)} all-to-all(bf16[4,48,1,512]{3,1,2,0:T(8,128)(2,1)S(1)} %bitcast.85), channel_id=1, replica_groups=mesh['grp'=4,'seq'=8] {'grp'}, dimensions={0} | all-to-all | bytes 393216 | tf_op jit(solution)/shard_map/all_to_all | solution.py:122
  271.5 5.9 %reduce-scatter.14.cloned.1.call-done = bf16[48,1024]{1,0:T(8,128)(2,1)} async-done(((bf16[384,1024]{1,0:T(8,128)(2,1)}), bf16[48,1024]{1,0:T(8,128)(2,1)}) %reduce-scatter.14.cloned.1.call-update) | async-done | bytes 98320 | tf_op jit(solution)/shard_map/reduce_scatter | solution.py:100
  277.3 3.4 %collective-permute-start.1 = (bf16[48,1024]{1,0:T(8,128)(2,1)}, bf16[48,1024]{1,0:T(8,128)(2,1)S(1)}, u32[]{:S(2)}, u32[]{:S(2)}) collective-permute-start(bf16[48,1024]{1,0:T(8,128)(2,1)} %reduce-scatter.14.cloned.1.call-done), channel_id=1, source_target_pairs={{0,0},{1,1},{2,8},{3,9},{4,16},{5,17},{6,24},{7,25},{8,2},{9,3},{1... | collective-permute-start | bytes 294920 | tf_op jit(solution)/shard_map/ppermute | solution.py:48
  280.7 8.1 %collective-permute-done.1 = bf16[48,1024]{1,0:T(8,128)(2,1)S(1)} collective-permute-done((bf16[48,1024]{1,0:T(8,128)(2,1)}, bf16[48,1024]{1,0:T(8,128)(2,1)S(1)}, u32[]{:S(2)}, u32[]{:S(2)}) %collective-permute-start.1) | collective-permute-done | bytes 98336 | tf_op jit(solution)/shard_map/ppermute | solution.py:48
  289.7 25.1 %reduce-scatter.20.cloned.1.call-done = bf16[8,2048]{1,0:T(8,128)(2,1)} async-done(((bf16[64,2048]{1,0:T(8,128)(2,1)}), bf16[8,2048]{1,0:T(8,128)(2,1)}) %reduce-scatter.20.cloned.1.call-update) | async-done | bytes 32784 | tf_op jit(solution)/shard_map/reduce_scatter | solution.py:126
  315.7 1.9 fusion.1
  (59 shorter events, 17.1 us)
Async XLA Ops:
  7.2 32.1 %copy-start = (bf16[512,1024]{1,0:T(8,128)(2,1)S(1)}, bf16[512,1024]{1,0:T(8,128)(2,1)}, u32[]{:S(2)}) copy-start(bf16[512,1024]{1,0:T(8,128)(2,1)} %param.11) | copy-start | bytes 3145732
  23.1 12.9 %all-to-all-start = ((bf16[1,48,4,512]{3,1,0,2:T(8,128)(2,1)}), bf16[1,48,4,512]{3,1,0,2:T(8,128)(2,1)S(1)}, u32[]{:S(2)}, u32[]{:S(2)}) async-start(bf16[1,48,4,512]{3,1,0,2:T(8,128)(2,1)} %copy.18), calls=%async_computation | async-start | bytes 393216 | tf_op jit(solution)/shard_map/all_to_all | solution.py:75
  35.9 9.1 %all-to-all-start.1 = ((bf16[1,48,4,256]{3,1,0,2:T(8,128)(2,1)}), bf16[1,48,4,256]{3,1,0,2:T(8,128)(2,1)S(1)}, u32[]{:S(2)}, u32[]{:S(2)}) async-start(bf16[1,48,4,256]{3,1,0,2:T(8,128)(2,1)} %copy.22), calls=%async_computation.5 | async-start | bytes 196608 | tf_op jit(solution)/shard_map/all_to_all | solution.py:86
  39.2 25.2 %reduce-scatter.8.cloned.1.call-start = ((), (), s32[]{:S(2)}) async-start(), calls=%async_computation.10 | async-start | bytes 491520 | tf_op jit(solution)/shard_map/reduce_scatter | solution.py:38
  40.4 65.1 %reduce-scatter.16.cloned.1.call-start = ((), (), s32[]{:S(2)}) async-start(), calls=%async_computation.14 | async-start | bytes 983040 | tf_op jit(solution)/shard_map/reduce_scatter | solution.py:38
  64.4 56.4 %reduce-scatter.10.cloned.1.call-start = ((), (), s32[]{:S(2)}) async-start(), calls=%async_computation.11 | async-start | bytes 983040 | tf_op jit(solution)/shard_map/reduce_scatter | solution.py:38
  64.5 18.2 %collective-permute-start = (bf16[48,1024]{1,0:T(8,128)(2,1)}, bf16[48,1024]{1,0:T(8,128)(2,1)S(1)}, u32[]{:S(2)}, u32[]{:S(2)}) collective-permute-start(bf16[48,1024]{1,0:T(8,128)(2,1)} %reduce-scatter.8.cloned.1.call-done), channel_id=1, source_target_pairs={{0,0},{1,1},{2,8},{3,9},{4,16},{5,17},{6,24},{7,25},{8,2},{9,3},{1... | collective-permute-start | bytes 294920 | tf_op jit(solution)/shard_map/ppermute | solution.py:48
  99.3 46.4 %reduce-scatter.12.cloned.1.call-start = ((), (), s32[]{:S(2)}) async-start(), calls=%async_computation.12 | async-start | bytes 983040 | tf_op jit(solution)/shard_map/reduce_scatter | solution.py:38
  105.5 126.4 %reduce-scatter.18.cloned.1.call-start = ((), (), s32[]{:S(2)}) async-start(), calls=%async_computation.15 | async-start | bytes 884736 | tf_op jit(solution)/shard_map/reduce_scatter | solution.py:100
  196.9 80.4 %reduce-scatter.14.cloned.1.call-start = ((), (), s32[]{:S(2)}) async-start(), calls=%async_computation.13 | async-start | bytes 884736 | tf_op jit(solution)/shard_map/reduce_scatter | solution.py:100
  213.7 75.0 %copy-start.1 = (bf16[48,1024]{1,0:T(8,128)(2,1)S(1)}, bf16[48,1024]{1,0:T(8,128)(2,1)}, u32[]{:S(2)}) copy-start(bf16[48,1024]{1,0:T(8,128)(2,1)} %reduce-scatter.8.cloned.1.call-done) | copy-start | bytes 294916
  231.9 11.5 %collective-permute-start.2 = (bf16[48,1024]{1,0:T(8,128)(2,1)}, bf16[48,1024]{1,0:T(8,128)(2,1)S(1)}, u32[]{:S(2)}, u32[]{:S(2)}) collective-permute-start(bf16[48,1024]{1,0:T(8,128)(2,1)} %reduce-scatter.18.cloned.1.call-done), channel_id=1, source_target_pairs={{0,0},{1,1},{2,8},{3,9},{4,16},{5,17},{6,24},{7,25},{8,2},{9,3},{1... | collective-permute-start | bytes 294920 | tf_op jit(solution)/shard_map/ppermute | solution.py:48
  240.5 74.3 %copy-start.2 = (f32[2048]{0:T(1024)S(1)}, f32[2048]{0:T(1024)}, u32[]{:S(2)}) copy-start(f32[2048]{0:T(1024)} %param.10) | copy-start | bytes 24580
  240.5 75.2 %copy-start.3 = (s32[1,128]{1,0:T(1,128)S(1)}, s32[1,128]{1,0:T(1,128)}, u32[]{:S(2)}) copy-start(s32[1,128]{1,0:T(1,128)} %param.9) | copy-start | bytes 1540
  242.2 72.6 %reduce-scatter.20.cloned.1.call-start = ((), (), s32[]{:S(2)}) async-start(), calls=%async_computation.16 | async-start | bytes 294912 | tf_op jit(solution)/shard_map/reduce_scatter | solution.py:126
  277.3 11.5 %collective-permute-start.1 = (bf16[48,1024]{1,0:T(8,128)(2,1)}, bf16[48,1024]{1,0:T(8,128)(2,1)S(1)}, u32[]{:S(2)}, u32[]{:S(2)}) collective-permute-start(bf16[48,1024]{1,0:T(8,128)(2,1)} %reduce-scatter.14.cloned.1.call-done), channel_id=1, source_target_pairs={{0,0},{1,1},{2,8},{3,9},{4,16},{5,17},{6,24},{7,25},{8,2},{9,3},{1... | collective-permute-start | bytes 294920 | tf_op jit(solution)/shard_map/ppermute | solution.py:48
Sparse Core Ops, SparseCore 0:
  42.9 20.9 reduce-scatter.7
  66.4 21.7 reduce-scatter.15
  99.4 21.3 reduce-scatter.9
  123.1 22.5 reduce-scatter.11
  197.0 34.8 reduce-scatter.17
  242.3 34.9 reduce-scatter.13
  281.2 33.5 reduce-scatter.19

commit v2 on v1

v2 whole, which is shorter than its diff:
```python
import functools

import jax
import jax.numpy as jnp
from jax import lax
from jax.experimental import pallas as pl
from jax.experimental.pallas import tpu as pltpu
from jax.sharding import PartitionSpec as P

SEG_CAP = 8


norm_eps = 1e-06
bf16 = jnp.bfloat16
f32 = jnp.float32


def silu_parts(gate_value):
    sigma = jax.nn.sigmoid(gate_value)
    return (gate_value * sigma, sigma * (1.0 + gate_value * (1.0 - sigma)))


def matmul(a, b):
    return jnp.dot(a, b, preferred_element_type=f32)


def matmul_t(a, b):
    return lax.dot_general(a, b, (((1,), (1,)), ((), ())), preferred_element_type=f32)


def greet(axis, count):
    me = lax.axis_index(axis)
    barrier = pltpu.get_barrier_semaphore()
    for step in range(1, count):
        pl.semaphore_signal(
            barrier,
            inc=1,
            device_id={axis: lax.rem(me + step, count)},
            device_id_type=pl.DeviceIdType.MESH,
        )
    pl.semaphore_wait(barrier, count - 1)
    return me


def exchange_kernel(axis, count, modes, *refs):
    arrays = len(modes)
    ins, outs = refs[:arrays], refs[arrays : 2 * arrays]
    send_sem, recv_sem, own_sem = refs[2 * arrays :]
    me = greet(axis, count)
    copies = []
    for at, mode in enumerate(modes):
        for step in range(1, count):
            peer = lax.rem(me + step, count)
            copy = pltpu.make_async_remote_copy(
                src_ref=ins[at].at[peer] if mode == "swap" else ins[at],
                dst_ref=outs[at].at[me],
                send_sem=send_sem.at[at, step],
                recv_sem=recv_sem.at[at, step],
                device_id={axis: peer},
                device_id_type=pl.DeviceIdType.MESH,
            )
            copy.start()
            copies.append(copy)
        copy = pltpu.make_async_copy(
            ins[at].at[me] if mode == "swap" else ins[at], outs[at].at[me], own_sem.at[at]
        )
        copy.start()
        copies.append(copy)
    for copy in copies:
        copy.wait()


def exchange(arrays, axis, count, modes, ident):
    shapes = [a.shape if m == "swap" else (count,) + a.shape for a, m in zip(arrays, modes)]
    return pl.pallas_call(
        functools.partial(exchange_kernel, axis, count, modes),
        out_shape=[jax.ShapeDtypeStruct(sh, a.dtype) for sh, a in zip(shapes, arrays)],
        in_specs=[pl.BlockSpec(memory_space=pltpu.VMEM)] * len(arrays),
        out_specs=[pl.BlockSpec(memory_space=pltpu.VMEM)] * len(arrays),
        scratch_shapes=[
            pltpu.SemaphoreType.DMA((len(arrays), count)),
            pltpu.SemaphoreType.DMA((len(arrays), count)),
            pltpu.SemaphoreType.DMA((len(arrays),)),
        ],
        compiler_params=pltpu.CompilerParams(collective_id=ident, has_side_effects=True),
        name="exchange_%d" % ident,
    )(*arrays)


def block_kernel(
    grps, rows, tile, width, x_ref, gh_ref, gate_hbm, up_hbm, down_hbm, back_out, down_out,
    gate_w, up_w, down_w, part, part_in, held, back_acc, down_acc,
    load_sem, send_a, recv_a, send_b, recv_b,
):
    block, hidden_width = gate_w.shape
    tiles = hidden_width // tile
    col = back_acc.shape[2]
    cols = block // col
    loads = [
        pltpu.make_async_copy(src, dst, load_sem.at[at])
        for at, (src, dst) in enumerate(((gate_hbm, gate_w), (up_hbm, up_w), (down_hbm, down_w)))
    ]
    for load in loads:
        load.start()
    me = greet("grp", grps)

    def part_copy(t, step):
        peer = lax.rem(me + step, grps)
        return pltpu.make_async_remote_copy(
            src_ref=part.at[t, peer],
            dst_ref=part_in.at[t, step - 1],
            send_sem=send_a.at[t, step],
            recv_sem=recv_a.at[t, step],
            device_id={"grp": peer},
            device_id_type=pl.DeviceIdType.MESH,
        )

    def held_copy(t, step):
        return pltpu.make_async_remote_copy(
            src_ref=held.at[t, me],
            dst_ref=held.at[t, me],
            send_sem=send_b.at[t, step],
            recv_sem=recv_b.at[t, step],
            device_id={"grp": lax.rem(me + step, grps)},
            device_id_type=pl.DeviceIdType.MESH,
        )

    loads[0].wait()
    loads[1].wait()

    @pl.loop(0, tiles)
    def _(t):
        here = pl.ds(pl.multiple_of(t * tile, tile), tile)
        for at, weight in enumerate((gate_w, up_w)):
            value = matmul(x_ref[...], weight[:, here]).astype(bf16)
            part[t, :, at] = value.reshape(grps, rows, tile)
        for step in range(1, grps):
            part_copy(t, step).start()

    @pl.loop(0, tiles)
    def _(t):
        gate_value = part[t, me, 0].astype(f32)
        up_value = part[t, me, 1].astype(f32)
        for step in range(1, grps):
            part_copy(t, step).wait_recv()
            gate_value = gate_value + part_in[t, step - 1, 0].astype(f32)
            up_value = up_value + part_in[t, step - 1, 1].astype(f32)
        grad_hidden = gh_ref[:, pl.ds(pl.multiple_of(t * tile, tile), tile)]
        activated, derivative = silu_parts(gate_value)
        held[t, me, 0] = (grad_hidden * up_value * derivative).astype(bf16)
        held[t, me, 1] = (grad_hidden * activated).astype(bf16)
        held[t, me, 2] = (activated * up_value).astype(bf16)
        for step in range(1, grps):
            held_copy(t, step).start()

    loads[2].wait()

    @pl.loop(0, tiles)
    def _(t):
        here = pl.ds(pl.multiple_of(t * tile, tile), tile)
        for step in range(1, grps):
            held_copy(t, step).wait_recv()
        grad_gate = held[t, :, 0].reshape(grps * rows, tile)
        grad_up = held[t, :, 1].reshape(grps * rows, tile)
        hidden = held[t, :, 2].reshape(grps * rows, tile)

        @pl.loop(0, cols)
        def _(c):
            there = pl.ds(pl.multiple_of(c * col, col), col)
            back = matmul_t(grad_gate, gate_w[there, here]) + matmul_t(grad_up, up_w[there, here])
            down = matmul(hidden, down_w[here, there])

            @pl.when(t == 0)
            def _():
                back_acc[c] = back
                down_acc[c] = down

            @pl.when(t > 0)
            def _():
                back_acc[c] += back
                down_acc[c] += down

    halves = block // width
    fits = width // col
    for c in range(cols):
        half, at = c // fits, c % fits
        for acc, out in ((back_acc, back_out), (down_acc, down_out)):
            value = acc[c].astype(bf16)
            for g in range(grps):
                out[g * halves + half, :, at * col : (at + 1) * col] = value[
                    g * rows : (g + 1) * rows
                ]

    @pl.loop(0, tiles)
    def _(t):
        for step in range(1, grps):
            part_copy(t, step).wait_send()
            held_copy(t, step).wait_send()


def coarse_block(coarse_x, grad_hidden, w_gate, w_up, w_down, grps, rows, width, ident):
    block, hidden_width = w_gate.shape
    tile = min(512, hidden_width)
    tiles = hidden_width // tile
    col = min(512, width)
    seqs = grps * (block // width)
    vmem = pl.BlockSpec(memory_space=pltpu.VMEM)
    hbm = pl.BlockSpec(memory_space=pl.ANY)
    return pl.pallas_call(
        functools.partial(block_kernel, grps, rows, tile, width),
        out_shape=[jax.ShapeDtypeStruct((seqs, rows, width), bf16)] * 2,
        in_specs=[vmem, vmem, hbm, hbm, hbm],
        out_specs=[vmem, vmem],
        scratch_shapes=[
            pltpu.VMEM(w_gate.shape, bf16),
            pltpu.VMEM(w_up.shape, bf16),
            pltpu.VMEM(w_down.shape, bf16),
            pltpu.VMEM((tiles, grps, 2, rows, tile), bf16),
            pltpu.VMEM((tiles, grps - 1, 2, rows, tile), bf16),
            pltpu.VMEM((tiles, grps, 3, rows, tile), bf16),
            pltpu.VMEM((block // col, grps * rows, col), f32),
            pltpu.VMEM((block // col, grps * rows, col), f32),
            pltpu.SemaphoreType.DMA((3,)),
        ]
        + [pltpu.SemaphoreType.DMA((tiles, grps))] * 4,
        compiler_params=pltpu.CompilerParams(
            collective_id=ident, has_side_effects=True, vmem_limit_bytes=56 * 2**20
        ),
        name="coarse_block",
    )(coarse_x, grad_hidden, w_gate, w_up, w_down)


def swap_pairs(grps, seqs):
    halves = seqs // grps
    return [
        (g * seqs + p * halves + h, p * seqs + g * halves + h)
        for g in range(grps)
        for p in range(grps)
        for h in range(halves)
    ]


def grp_total(partial_value):
    return lax.psum_scatter(
        partial_value.astype(bf16), "grp", scatter_dimension=0, tiled=True
    ).astype(f32)


def make_shards(grps, seqs):
    halves = seqs // grps
    pairs = swap_pairs(grps, seqs)

    def swap(value):
        return lax.ppermute(value, ("grp", "seq"), pairs)

    def shards(fine_rows, segment_ids, pool_gain, w_in, w_gate, w_up, w_down, out_grad):
        rows_here = fine_rows[0]
        index_here = segment_ids[0]
        feat, width = w_in.shape
        slots = jnp.arange(SEG_CAP, dtype=jnp.int32)
        member = index_here[None, :] == slots[:, None]
        segment_sums = matmul(member.astype(bf16), rows_here)
        inv_rms = lax.rsqrt(jnp.mean(segment_sums * segment_sums, axis=1, keepdims=True) + norm_eps)
        pooled = (segment_sums * inv_rms * pool_gain).astype(bf16)
        live_count = jnp.max(index_here) + 1
        packed = jnp.concatenate(
            [pooled, jnp.full(pooled.shape, live_count.astype(bf16))], axis=0
        )
        gathered = exchange([packed], "seq", seqs, ("share",), 0)[0]
        shard_counts = gathered[:, SEG_CAP, 0].astype(jnp.int32)
        gathered = gathered[:, :SEG_CAP].reshape(seqs * SEG_CAP, -1)
        offsets = jnp.cumsum(shard_counts) - shard_counts
        slot_count = seqs * SEG_CAP
        within = jnp.tile(slots, seqs)
        target = jnp.repeat(offsets, SEG_CAP) + within
        is_live = within < jnp.repeat(shard_counts, SEG_CAP)
        rows = slot_count * 3 // 4
        select = (target[None, :] == jnp.arange(rows, dtype=jnp.int32)[:, None]) & is_live[None, :]
        selector = select.astype(bf16)
        work_in = matmul(selector, gathered).astype(bf16)
        seq_at = lax.axis_index("seq")
        block = w_gate.shape[0]
        piece = block // seqs
        grad_here = out_grad[0].reshape(slot_count, grps, seqs, piece)
        grad_part = lax.dynamic_index_in_dim(grad_here, seq_at, 2, keepdims=False)
        grad_part = matmul(selector, grad_part.reshape(slot_count, grps * piece)).astype(bf16)
        work_in, grad_part = exchange(
            [
                work_in.reshape(rows, grps, feat).transpose(1, 0, 2),
                grad_part.reshape(rows, grps, piece).transpose(1, 0, 2),
            ],
            "grp",
            grps,
            ("swap", "swap"),
            1,
        )
        x_part = matmul(work_in.reshape(grps * rows, feat), w_in).astype(bf16)
        x_part = exchange([x_part.reshape(grps, rows, width)], "grp", grps, ("swap",), 2)[0]
        x_cols = jnp.sum(x_part.astype(f32), axis=0).astype(bf16)
        work_grad = exchange(
            [grad_part.reshape(grps * rows, piece)], "seq", seqs, ("share",), 3
        )[0]
        work_grad = work_grad.transpose(1, 0, 2).reshape(grps * rows, block)
        grad_hidden = grp_total(matmul_t(work_grad, w_down))

        def spread(cols):
            every = exchange([swap(cols)], "seq", seqs, ("share",), 4)[0]
            every = every.reshape(grps, halves, rows, width)
            return every.transpose(0, 2, 1, 3).reshape(grps * rows, halves * width)

        coarse_x = spread(x_cols)
        back_part, down_part = coarse_block(
            coarse_x, grad_hidden, w_gate, w_up, w_down, grps, rows, width, 5
        )
        back_in, down_in = exchange([back_part, down_part], "seq", seqs, ("swap", "swap"), 6)
        back_cols = swap(jnp.sum(back_in.astype(f32), axis=0).astype(bf16)).astype(f32)
        down_cols = swap(jnp.sum(down_in.astype(f32), axis=0).astype(bf16)).astype(f32)
        out_cols = (x_cols.astype(f32) + down_cols).astype(bf16)
        out_cols = matmul(selector.T, out_cols).astype(bf16)

        grad_cols = lax.dynamic_slice_in_dim(out_grad[0], seq_at * width, width, 1)
        grad_cols = matmul(selector, grad_cols)
        grad_x = (back_cols + grad_cols).astype(bf16)
        grad_x = exchange([grad_x], "grp", grps, ("share",), 7)[0].reshape(grps * rows, width)
        term = matmul_t(grad_x, w_in).astype(bf16)
        term = exchange([term.reshape(grps, rows, feat)], "grp", grps, ("swap",), 8)[0]
        term = term.transpose(1, 0, 2).reshape(rows, grps * feat)
        term = matmul(selector.T, term).astype(bf16).reshape(seqs, SEG_CAP, grps * feat)
        term = exchange([term], "seq", seqs, ("swap",), 9)[0]
        grad_pooled = jnp.sum(term.astype(f32), axis=0)
        weighted = grad_pooled * pool_gain
        inner = jnp.mean(weighted * segment_sums, axis=1, keepdims=True)
        grad_sums = inv_rms * weighted - segment_sums * (inv_rms * inv_rms * inv_rms) * inner
        fine_grad = matmul(member.astype(bf16).T, grad_sums.astype(bf16)).astype(bf16)
        return (out_cols[None], fine_grad[None])

    return shards


def solution(mesh):
    return jax.shard_map(
        make_shards(mesh.shape["grp"], mesh.shape["seq"]),
        mesh=mesh,
        in_specs=(
            P("grp", "seq", None),
            P("grp", "seq"),
            P(),
            P("grp", "seq"),
            P("grp", "seq"),
            P("grp", "seq"),
            P("seq", "grp"),
            P("grp", None, None),
        ),
        out_specs=(P("grp", None, "seq"), P("grp", "seq", None)),
        check_vma=False,
    )
```

time: 327 us -> 304 us (0.930)
  Pallas kernels: 0 us -> 220 us
  waiting for transfers between devices: 123 us -> 9.61 us
  blocking collectives: 109 us -> 0 us
  matrix products: 45.5 us -> 17.9 us
  other arithmetic: 4.91 us -> 9.86 us
    pallas_call x0 -> x10, Pallas kernels: none -> 220 us  [the longest x9 125 us: exchange(): pl.pallas_call(functools.partial(exchange_kernel, axis, count, modes), ou...]
    all_gather x7 -> x0, blocking collectives: 99.2 us -> none  [the longest x1 18.2 us: shards(): grad_gate = lax.all_gather(grad_gate, 'grp', axis=0, tiled=True)]
    reduce_scatter x3 -> x0, waiting for transfers between devices: 49.1 us -> none  [the longest x1 25.1 us: shards(): lax.psum_scatter(term, 'seq', scatter_dimension=0, tiled=True).astype(f32)]
    reduce_scatter x4 -> x1, waiting for transfers between devices: 40.2 us -> 0.01 us  [grp_total(): lax.psum_scatter(partial_value.astype(bf16), 'grp', scatter_dimension=0,...]
    dot_general x11 -> x8, matrix products: 25.1 us -> 8.53 us  [matmul(): return jnp.dot(a, b, preferred_element_type=f32)]
    ppermute x3, waiting for transfers between devices: 24.4 us -> 9.59 us  [swap(): return lax.ppermute(value, ('grp', 'seq'), pairs)]
    dot_general x4 -> x2, matrix products: 20.3 us -> 9.38 us  [matmul_t(): lax.dot_general(a, b, (((1,), (1,)), ((), ())), preferred_element_type=f32)]
    all_to_all x1 -> x0, blocking collectives: 10.1 us -> none  [shards(): lax.all_to_all(term.reshape(grps, rows, feat), 'grp', split_axis=0, conca...]
  transfers between devices with their start and end apart: 12 -> 4, of which waited for: 10 -> 2; matrix products, arithmetic and copies ran while one was open for 11% -> 5% of each run, Pallas kernels for 0% -> 22%
where the time goes in v2:
time: 304 us; the launch traced here: 300 us
  Pallas kernels  220 us (72%)
  matrix products  17.9 us (6%)
  starting transfers between devices  17.8 us (6%)
  between operations  14.9 us (5%)
  local copies, waits for them, and re-layouts  10.3 us (3%)
  other arithmetic  9.86 us (3%)
  waiting for transfers between devices  9.61 us (3%)
    pallas_call x9, Pallas kernels, exchange(): pl.pallas_call(functools.partial(exchange_kernel, axis, count, modes), ou...  125 us
    pallas_call x1, Pallas kernels, coarse_block(): pl.pallas_call(functools.partial(block_kernel, grps, rows, tile, width),...  94.7 us
    ppermute x3, starting transfers between devices, swap(): return lax.ppermute(value, ('grp', 'seq'), pairs)  17.8 us
    ppermute x3, waiting for transfers between devices, swap(): return lax.ppermute(value, ('grp', 'seq'), pairs)  9.59 us
    dot_general x2, matrix products, matmul_t(): lax.dot_general(a, b, (((1,), (1,)), ((), ())), preferred_element_type=f32)  9.38 us
    dot_general x8, matrix products, matmul(): return jnp.dot(a, b, preferred_element_type=f32)  8.53 us
  transfers between devices with their start and end apart: 4, of which 2 were waited for; matrix products, arithmetic and copies ran while one was open for 5% of the time, Pallas kernels for 22%

profile of v2, /device:TPU:2, one launch (start us, length us, event | category | flops | bytes accessed | tf_op | source)
XLA Modules:
  0.0 300.0 jit_solution(15168420044764899538)
XLA Ops:
  7.2 1.4 reduce_max.9
  9.3 1.4 multiply_reduce_fusion.1
  12.0 10.4 %exchange_0.1 = bf16[8,16,2048]{2,1,0:T(8,128)(2,1)} custom-call(bf16[16,2048]{1,0:T(8,128)(2,1)} %concatenate.3.refs_0_), custom_call_target="tpu_custom_call" | custom-call | tf_op jit(solution)/shard_map/exchange_0/pallas_call | solution.py:75
  24.0 1.2 convolution_convert_fusion.3
  25.8 1.5 copy.22
  28.9 13.1 %exchange_1.1 = (bf16[4,48,512]{2,1,0:T(8,128)(2,1)}, bf16[4,48,256]{2,1,0:T(8,128)(2,1)}) custom-call(bf16[4,48,512]{2,1,0:T(8,128)(2,1)} %bitcast.79, bf16[4,48,256]{2,1,0:T(8,128)(2,1)} %bitcast.84), custom_call_target="tpu_custom_call" | custom-call | tf_op jit(solution)/shard_map/exchange_1/pallas_call | solution.py:75
  42.0 12.7 %exchange_3.1 = bf16[8,192,256]{2,1,0:T(8,128)(2,1)} custom-call(bf16[192,256]{1,0:T(8,128)(2,1)} %bitcast.86), custom_call_target="tpu_custom_call" | custom-call | tf_op jit(solution)/shard_map/exchange_3/pallas_call | solution.py:75
  54.7 1.2 copy.20
  55.9 7.2 %convolution_convert_fusion = bf16[192,2048]{1,0:T(8,128)(2,1)} fusion(bf16[192,2048]{1,0:T(8,128)(2,1)S(1)} %bitcast.78, bf16[2048,2048]{1,0:T(8,128)(2,1)} %down_hbm.1), kind=kOutput, calls=%fused_computation | convolution fusion | flops 1611005952 | bytes 9961472 | tf_op jit(solution)/shard_map/dot_general | solution.py:28
  63.2 1.1 convolution_convert_fusion.4
  64.3 16.3 %exchange_2.1 = bf16[4,48,1024]{2,1,0:T(8,128)(2,1)} custom-call(bf16[4,48,1024]{2,1,0:T(8,128)(2,1)} %bitcast.72), custom_call_target="tpu_custom_call" | custom-call | tf_op jit(solution)/shard_map/exchange_2/pallas_call | solution.py:75
  80.6 1.1 reduce_sum.64
  81.7 10.8 %collective-permute-start = (bf16[48,1024]{1,0:T(8,128)(2,1)S(1)}, bf16[48,1024]{1,0:T(8,128)(2,1)S(1)}, u32[]{:S(2)}, u32[]{:S(2)}) collective-permute-start(bf16[48,1024]{1,0:T(8,128)(2,1)S(1)} %reduce_sum.64), channel_id=1, source_target_pairs={{0,0},{1,1},{2,8},{3,9},{4,16},{5,17},{6,24},{7,25},{8,2},{9,3},{1... | collective-permute-start | bytes 294920 | tf_op jit(solution)/shard_map/ppermute | solution.py:254
  92.5 5.4 %collective-permute-done.refs_0_ = bf16[48,1024]{1,0:T(8,128)(2,1)S(1)} collective-permute-done((bf16[48,1024]{1,0:T(8,128)(2,1)S(1)}, bf16[48,1024]{1,0:T(8,128)(2,1)S(1)}, u32[]{:S(2)}, u32[]{:S(2)}) %collective-permute-start) | collective-permute-done | bytes 98336 | tf_op jit(solution)/shard_map/ppermute | solution.py:254
  98.6 12.7 %exchange_4.1 = bf16[8,48,1024]{2,1,0:T(8,128)(2,1)} custom-call(bf16[48,1024]{1,0:T(8,128)(2,1)} %copy-done.2), custom_call_target="tpu_custom_call" | custom-call | tf_op jit(solution)/shard_map/exchange_4/pallas_call | solution.py:75
  111.2 1.9 copy.14
  113.2 1.1 copy.24
  114.3 1.7 convert_element_type.92.gh_ref
  116.0 94.7 %coarse_block.1 = (bf16[8,48,1024]{2,1,0:T(8,128)(2,1)}, bf16[8,48,1024]{2,1,0:T(8,128)(2,1)}) custom-call(bf16[192,2048]{1,0:T(8,128)(2,1)} %bitcast.67, f32[48,2048]{1,0:T(8,128)} %convert_element_type.92.gh_ref, bf16[2048,2048]{1,0:T(8,128)(2,1)} %gate_hbm.1, bf16[2048,2048]{1,0:T(8,128)(2,1)} %up_hbm.1, bf16[2048,2048]{1,0:T(8,128)(2,1)} %down_hbm.1), custom_call_target="tpu_custom_call" | custom-call | tf_op jit(solution)/shard_map/coarse_block/pallas_call | solution.py:209
  210.7 22.9 %exchange_6.1 = (bf16[8,48,1024]{2,1,0:T(8,128)(2,1)}, bf16[8,48,1024]{2,1,0:T(8,128)(2,1)}) custom-call(bf16[8,48,1024]{2,1,0:T(8,128)(2,1)} %get-tuple-element.10.refs_0_, bf16[8,48,1024]{2,1,0:T(8,128)(2,1)} %get-tuple-element.11.refs_1_), custom_call_target="tpu_custom_call" | custom-call | tf_op jit(solution)/shard_map/exchange_6/pallas_call | solution.py:75
  233.6 1.3 reduce_sum.66
  234.8 5.0 %collective-permute-start.2 = (bf16[48,1024]{1,0:T(8,128)(2,1)S(1)}, bf16[48,1024]{1,0:T(8,128)(2,1)S(1)}, u32[]{:S(2)}, u32[]{:S(2)}) collective-permute-start(bf16[48,1024]{1,0:T(8,128)(2,1)S(1)} %reduce_sum.66), channel_id=1, source_target_pairs={{0,0},{1,1},{2,8},{3,9},{4,16},{5,17},{6,24},{7,25},{8,2},{9,3},{1... | collective-permute-start | bytes 294920 | tf_op jit(solution)/shard_map/ppermute | solution.py:254
  239.8 1.3 reduce_sum.65
  241.1 1.9 collective-permute-start.1
  243.0 4.2 %collective-permute-done.2 = bf16[48,1024]{1,0:T(8,128)(2,1)S(1)} collective-permute-done((bf16[48,1024]{1,0:T(8,128)(2,1)S(1)}, bf16[48,1024]{1,0:T(8,128)(2,1)S(1)}, u32[]{:S(2)}, u32[]{:S(2)}) %collective-permute-start.2) | collective-permute-done | bytes 98336 | tf_op jit(solution)/shard_map/ppermute | solution.py:254
  247.2 1.7 add_convert_fusion.refs_0_
  248.9 14.6 %exchange_7.1 = bf16[4,48,1024]{2,1,0:T(8,128)(2,1)} custom-call(bf16[48,1024]{1,0:T(8,128)(2,1)} %add_convert_fusion.refs_0_), custom_call_target="tpu_custom_call" | custom-call | tf_op jit(solution)/shard_map/exchange_7/pallas_call | solution.py:75
  263.6 2.2 convolution_convert_fusion.5
  265.8 10.0 %exchange_8.1 = bf16[4,48,512]{2,1,0:T(8,128)(2,1)} custom-call(bf16[4,48,512]{2,1,0:T(8,128)(2,1)} %bitcast.76), custom_call_target="tpu_custom_call" | custom-call | tf_op jit(solution)/shard_map/exchange_8/pallas_call | solution.py:75
  277.7 12.2 %exchange_9.1 = bf16[8,8,2048]{2,1,0:T(8,128)(2,1)} custom-call(bf16[8,8,2048]{2,1,0:T(8,128)(2,1)} %fusion.1.refs_0_), custom_call_target="tpu_custom_call" | custom-call | tf_op jit(solution)/shard_map/exchange_9/pallas_call | solution.py:75
  289.9 1.0 convert_reduce_fusion
  291.1 1.2 fusion
  (34 shorter events, 8.9 us)
Async XLA Ops:
  7.2 56.0 %copy-start = (bf16[512,1024]{1,0:T(8,128)(2,1)S(1)}, bf16[512,1024]{1,0:T(8,128)(2,1)}, u32[]{:S(2)}) copy-start(bf16[512,1024]{1,0:T(8,128)(2,1)} %param.11) | copy-start | bytes 3145732
  7.2 107.1 %reduce-scatter.2.cloned.1.call-start = ((), (), s32[]{:S(2)}) async-start(), calls=%async_computation.1 | async-start | bytes 983040 | tf_op jit(solution)/shard_map/reduce_scatter | solution.py:244
  42.0 21.1 %copy-start.1 = (bf16[4,48,512]{2,1,0:T(8,128)(2,1)S(1)}, bf16[4,48,512]{2,1,0:T(8,128)(2,1)}, u32[]{:S(2)}) copy-start(bf16[4,48,512]{2,1,0:T(8,128)(2,1)} %get-tuple-element.8) | copy-start | bytes 589828
  81.7 16.2 %collective-permute-start = (bf16[48,1024]{1,0:T(8,128)(2,1)S(1)}, bf16[48,1024]{1,0:T(8,128)(2,1)S(1)}, u32[]{:S(2)}, u32[]{:S(2)}) collective-permute-start(bf16[48,1024]{1,0:T(8,128)(2,1)S(1)} %reduce_sum.64), channel_id=1, source_target_pairs={{0,0},{1,1},{2,8},{3,9},{4,16},{5,17},{6,24},{7,25},{8,2},{9,3},{1... | collective-permute-start | bytes 294920 | tf_op jit(solution)/shard_map/ppermute | solution.py:254
  97.9 0.6 copy-start.2
  116.0 174.9 %copy-start.3 = (f32[2048]{0:T(1024)S(1)}, f32[2048]{0:T(1024)}, u32[]{:S(2)}) copy-start(f32[2048]{0:T(1024)} %param.10) | copy-start | bytes 24580
  116.0 175.1 %copy-start.4 = (s32[1,128]{1,0:T(1,128)S(1)}, s32[1,128]{1,0:T(1,128)}, u32[]{:S(2)}) copy-start(s32[1,128]{1,0:T(1,128)} %param.9) | copy-start | bytes 1540
  234.8 12.4 %collective-permute-start.2 = (bf16[48,1024]{1,0:T(8,128)(2,1)S(1)}, bf16[48,1024]{1,0:T(8,128)(2,1)S(1)}, u32[]{:S(2)}, u32[]{:S(2)}) collective-permute-start(bf16[48,1024]{1,0:T(8,128)(2,1)S(1)} %reduce_sum.66), channel_id=1, source_target_pairs={{0,0},{1,1},{2,8},{3,9},{4,16},{5,17},{6,24},{7,25},{8,2},{9,3},{1... | collective-permute-start | bytes 294920 | tf_op jit(solution)/shard_map/ppermute | solution.py:254
  241.1 51.1 %collective-permute-start.1 = (bf16[48,1024]{1,0:T(8,128)(2,1)S(1)}, bf16[48,1024]{1,0:T(8,128)(2,1)S(1)}, u32[]{:S(2)}, u32[]{:S(2)}) collective-permute-start(bf16[48,1024]{1,0:T(8,128)(2,1)S(1)} %reduce_sum.65), channel_id=1, source_target_pairs={{0,0},{1,1},{2,8},{3,9},{4,16},{5,17},{6,24},{7,25},{8,2},{9,3},{1... | collective-permute-start | bytes 294920 | tf_op jit(solution)/shard_map/ppermute | solution.py:254
Sparse Core Ops, SparseCore 0:
  63.3 29.3 reduce-scatter.1

commit v3 on v2

--- a/solution.py
+++ b/solution.py
@@ -257,6 +257,7 @@
         rows_here = fine_rows[0]
         index_here = segment_ids[0]
         feat, width = w_in.shape
+        full_in = lax.all_gather(w_in, "grp", axis=0, tiled=True)
         slots = jnp.arange(SEG_CAP, dtype=jnp.int32)
         member = index_here[None, :] == slots[:, None]
         segment_sums = matmul(member.astype(bf16), rows_here)
@@ -264,11 +265,11 @@
         pooled = (segment_sums * inv_rms * pool_gain).astype(bf16)
         live_count = jnp.max(index_here) + 1
         packed = jnp.concatenate(
-            [pooled, jnp.full(pooled.shape, live_count.astype(bf16))], axis=0
+            [pooled, jnp.full((SEG_CAP, 128), live_count.astype(bf16))], axis=1
         )
         gathered = exchange([packed], "seq", seqs, ("share",), 0)[0]
-        shard_counts = gathered[:, SEG_CAP, 0].astype(jnp.int32)
-        gathered = gathered[:, :SEG_CAP].reshape(seqs * SEG_CAP, -1)
+        shard_counts = gathered[:, 0, -1].astype(jnp.int32)
+        gathered = gathered[:, :, :-128].reshape(seqs * SEG_CAP, -1)
         offsets = jnp.cumsum(shard_counts) - shard_counts
         slot_count = seqs * SEG_CAP
         within = jnp.tile(slots, seqs)
@@ -284,23 +285,15 @@
         grad_here = out_grad[0].reshape(slot_count, grps, seqs, piece)
         grad_part = lax.dynamic_index_in_dim(grad_here, seq_at, 2, keepdims=False)
         grad_part = matmul(selector, grad_part.reshape(slot_count, grps * piece)).astype(bf16)
-        work_in, grad_part = exchange(
-            [
-                work_in.reshape(rows, grps, feat).transpose(1, 0, 2),
-                grad_part.reshape(rows, grps, piece).transpose(1, 0, 2),
-            ],
-            "grp",
-            grps,
-            ("swap", "swap"),
-            1,
-        )
-        x_part = matmul(work_in.reshape(grps * rows, feat), w_in).astype(bf16)
-        x_part = exchange([x_part.reshape(grps, rows, width)], "grp", grps, ("swap",), 2)[0]
-        x_cols = jnp.sum(x_part.astype(f32), axis=0).astype(bf16)
+        grad_part = exchange(
+            [grad_part.reshape(rows, grps, piece).transpose(1, 0, 2)], "grp", grps, ("swap",), 1
+        )[0]
         work_grad = exchange(
             [grad_part.reshape(grps * rows, piece)], "seq", seqs, ("share",), 3
         )[0]
         work_grad = work_grad.transpose(1, 0, 2).reshape(grps * rows, block)
+        work_in, work_grad = lax.optimization_barrier((work_in, work_grad))
+        x_cols = matmul(work_in, full_in).astype(bf16)
         grad_hidden = grp_total(matmul_t(work_grad, w_down))
 
         def spread(cols):
@@ -312,20 +305,20 @@
         back_part, down_part = coarse_block(
             coarse_x, grad_hidden, w_gate, w_up, w_down, grps, rows, width, 5
         )
-        back_in, down_in = exchange([back_part, down_part], "seq", seqs, ("swap", "swap"), 6)
+        back_in = exchange([back_part], "seq", seqs, ("swap",), 6)[0]
         back_cols = swap(jnp.sum(back_in.astype(f32), axis=0).astype(bf16)).astype(f32)
-        down_cols = swap(jnp.sum(down_in.astype(f32), axis=0).astype(bf16)).astype(f32)
+        down_in = lax.psum_scatter(
+            down_part.reshape(seqs * rows, width), "seq", scatter_dimension=0, tiled=True
+        )
+        down_cols = swap(down_in).astype(f32)
         out_cols = (x_cols.astype(f32) + down_cols).astype(bf16)
         out_cols = matmul(selector.T, out_cols).astype(bf16)
 
         grad_cols = lax.dynamic_slice_in_dim(out_grad[0], seq_at * width, width, 1)
         grad_cols = matmul(selector, grad_cols)
         grad_x = (back_cols + grad_cols).astype(bf16)
-        grad_x = exchange([grad_x], "grp", grps, ("share",), 7)[0].reshape(grps * rows, width)
-        term = matmul_t(grad_x, w_in).astype(bf16)
-        term = exchange([term.reshape(grps, rows, feat)], "grp", grps, ("swap",), 8)[0]
-        term = term.transpose(1, 0, 2).reshape(rows, grps * feat)
-        term = matmul(selector.T, term).astype(bf16).reshape(seqs, SEG_CAP, grps * feat)
+        grad_x = matmul(selector.T, grad_x).astype(bf16)
+        term = matmul_t(grad_x, full_in).astype(bf16).reshape(seqs, SEG_CAP, grps * feat)
         term = exchange([term], "seq", seqs, ("swap",), 9)[0]
         grad_pooled = jnp.sum(term.astype(f32), axis=0)
         weighted = grad_pooled * pool_gain

time: 304 us -> 301 us (level)
  waiting for transfers between devices: 9.61 us -> 72.5 us
  Pallas kernels: 220 us -> 166 us
  starting transfers between devices: 17.8 us -> 10.9 us
    pallas_call x9 -> x6, Pallas kernels: 125 us -> 70.8 us  [exchange(): pl.pallas_call(functools.partial(exchange_kernel, axis, count, modes), ou...]
    all_gather x0 -> x1, waiting for transfers between devices: none -> 37.3 us  [shards(): full_in = lax.all_gather(w_in, 'grp', axis=0, tiled=True)]
    reduce_scatter x1, waiting for transfers between devices: 0.01 us -> 19.2 us  [grp_total(): lax.psum_scatter(partial_value.astype(bf16), 'grp', scatter_dimension=0,...]
    ppermute x3, starting transfers between devices: 17.8 us -> 10.8 us  [swap(): return lax.ppermute(value, ('grp', 'seq'), pairs)]
    ppermute x3, waiting for transfers between devices: 9.59 us -> 15.4 us  [swap(): return lax.ppermute(value, ('grp', 'seq'), pairs)]
    dot_general x8 -> x7, matrix products: 8.53 us -> 7.43 us  [matmul(): return jnp.dot(a, b, preferred_element_type=f32)]
  transfers between devices with their start and end apart: 4 -> 6, of which waited for: 2 -> 4; matrix products, arithmetic and copies ran while one was open for 5% -> 10% of each run, Pallas kernels for 22% -> 18%
where the time goes in v3:
time: 301 us; the launch traced here: 300 us
  Pallas kernels  166 us (55%)
  waiting for transfers between devices  72.5 us (24%)
  matrix products  19.1 us (6%)
  between operations  14.6 us (5%)
  starting transfers between devices  10.9 us (4%)
  local copies, waits for them, and re-layouts  8.67 us (3%)
  other arithmetic  7.6 us (3%)
    pallas_call x1, Pallas kernels, coarse_block(): pl.pallas_call(functools.partial(block_kernel, grps, rows, tile, width),...  95.6 us
    pallas_call x6, Pallas kernels, exchange(): pl.pallas_call(functools.partial(exchange_kernel, axis, count, modes), ou...  70.8 us
    all_gather x1, waiting for transfers between devices, shards(): full_in = lax.all_gather(w_in, 'grp', axis=0, tiled=True)  37.3 us
    reduce_scatter x1, waiting for transfers between devices, grp_total(): lax.psum_scatter(partial_value.astype(bf16), 'grp', scatter_dimension=0,...  19.2 us
    ppermute x3, waiting for transfers between devices, swap(): return lax.ppermute(value, ('grp', 'seq'), pairs)  15.4 us
    dot_general x2, matrix products, matmul_t(): lax.dot_general(a, b, (((1,), (1,)), ((), ())), preferred_element_type=f32)  11.6 us
    ppermute x3, starting transfers between devices, swap(): return lax.ppermute(value, ('grp', 'seq'), pairs)  10.8 us
    dot_general x7, matrix products, matmul(): return jnp.dot(a, b, preferred_element_type=f32)  7.43 us
  transfers between devices with their start and end apart: 6, of which 4 were waited for; matrix products, arithmetic and copies ran while one was open for 10% of the time, Pallas kernels for 18%

profile of v3, /device:TPU:2, one launch (start us, length us, event | category | flops | bytes accessed | tf_op | source)
XLA Modules:
  0.0 299.8 jit_solution(1073547060434493898)
XLA Ops:
  8.0 1.3 reduce_max.9
  9.9 1.0 multiply_reduce_fusion.1
  10.9 0.8 multiply_convert_fusion
  12.3 8.2 %exchange_0.1 = bf16[8,8,2176]{2,1,0:T(8,128)(2,1)} custom-call(bf16[8,2176]{1,0:T(8,128)(2,1)} %concatenate.3.refs_0_), custom_call_target="tpu_custom_call" | custom-call | tf_op jit(solution)/shard_map/exchange_0/pallas_call | solution.py:75
  20.5 1.1 convert_reduce_fusion.1
  22.1 1.5 copy.18
  23.6 0.8 dynamic-slice_reduce_fusion
  25.3 9.8 %exchange_1.1 = bf16[4,48,256]{2,1,0:T(8,128)(2,1)} custom-call(bf16[4,48,256]{2,1,0:T(8,128)(2,1)} %bitcast.64), custom_call_target="tpu_custom_call" | custom-call | tf_op jit(solution)/shard_map/exchange_1/pallas_call | solution.py:75
  35.1 12.7 %exchange_3.1 = bf16[8,192,256]{2,1,0:T(8,128)(2,1)} custom-call(bf16[192,256]{1,0:T(8,128)(2,1)} %bitcast.65), custom_call_target="tpu_custom_call" | custom-call | tf_op jit(solution)/shard_map/exchange_3/pallas_call | solution.py:75
  47.7 1.2 copy.17
  49.2 7.2 %convolution_convert_fusion = bf16[192,2048]{1,0:T(8,128)(2,1)} fusion(bf16[192,2048]{1,0:T(8,128)(2,1)S(1)} %bitcast.60, bf16[2048,2048]{1,0:T(8,128)(2,1)} %down_hbm.1), kind=kOutput, calls=%fused_computation | convolution fusion | flops 1611005952 | bytes 9961472 | tf_op jit(solution)/shard_map/dot_general | solution.py:28
  56.4 37.3 %all-gather.2.cloned.1.call-done = bf16[2048,1024]{1,0:T(8,128)(2,1)} async-done(((bf16[512,1024]{1,0:T(8,128)(2,1)}), bf16[2048,1024]{1,0:T(8,128)(2,1)}) %all-gather.2.cloned.1.call-update) | async-done | bytes 4194320 | tf_op jit(solution)/shard_map/all_gather | solution.py:260
  93.7 3.0 %convolution_convert_fusion.7 = bf16[48,1024]{1,0:T(8,128)(2,1)S(1)} fusion(bf16[48,2048]{1,0:T(8,128)(2,1)S(1)} %convolution_convert_fusion.3, bf16[2048,1024]{1,0:T(8,128)(2,1)} %all-gather.2.cloned.1.call-done), kind=kOutput, calls=%fused_computation.9 | convolution fusion | flops 201375744 | bytes 4489216 | tf_op jit(solution)/shard_map/dot_general | solution.py:24
  96.7 1.9 collective-permute-start
  98.7 19.2 %reduce-scatter.3.cloned.1.call-done = bf16[48,2048]{1,0:T(8,128)(2,1)} async-done(((bf16[192,2048]{1,0:T(8,128)(2,1)}), bf16[48,2048]{1,0:T(8,128)(2,1)}) %reduce-scatter.3.cloned.1.call-update) | async-done | bytes 196624 | tf_op jit(solution)/shard_map/reduce_scatter | solution.py:244
  117.8 1.7 convert_element_type.88.gh_ref
  120.2 18.0 %exchange_4.1 = bf16[8,48,1024]{2,1,0:T(8,128)(2,1)} custom-call(bf16[48,1024]{1,0:T(8,128)(2,1)} %copy-done.2), custom_call_target="tpu_custom_call" | custom-call | tf_op jit(solution)/shard_map/exchange_4/pallas_call | solution.py:75
  138.2 1.9 copy.14
  140.2 1.1 copy.20
  141.2 95.6 %coarse_block.1 = (bf16[8,48,1024]{2,1,0:T(8,128)(2,1)}, bf16[8,48,1024]{2,1,0:T(8,128)(2,1)}) custom-call(bf16[192,2048]{1,0:T(8,128)(2,1)} %bitcast.53, f32[48,2048]{1,0:T(8,128)} %convert_element_type.88.gh_ref, bf16[2048,2048]{1,0:T(8,128)(2,1)} %gate_hbm.1, bf16[2048,2048]{1,0:T(8,128)(2,1)} %up_hbm.1, bf16[2048,2048]{1,0:T(8,128)(2,1)} %down_hbm.1), custom_call_target="tpu_custom_call" | custom-call | tf_op jit(solution)/shard_map/coarse_block/pallas_call | solution.py:209
  236.9 13.8 %exchange_6.1 = bf16[8,48,1024]{2,1,0:T(8,128)(2,1)} custom-call(bf16[8,48,1024]{2,1,0:T(8,128)(2,1)} %get-tuple-element.9.refs_0_), custom_call_target="tpu_custom_call" | custom-call | tf_op jit(solution)/shard_map/exchange_6/pallas_call | solution.py:75
  250.7 1.3 reduce_sum.40
  251.9 5.8 %collective-permute-start.2 = (bf16[48,1024]{1,0:T(8,128)(2,1)S(1)}, bf16[48,1024]{1,0:T(8,128)(2,1)S(1)}, u32[]{:S(2)}, u32[]{:S(2)}) collective-permute-start(bf16[48,1024]{1,0:T(8,128)(2,1)S(1)} %reduce_sum.40), channel_id=1, source_target_pairs={{0,0},{1,1},{2,8},{3,9},{4,16},{5,17},{6,24},{7,25},{8,2},{9,3},{1... | collective-permute-start | bytes 294920 | tf_op jit(solution)/shard_map/ppermute | solution.py:254
  257.8 7.5 %collective-permute-done.2 = bf16[48,1024]{1,0:T(8,128)(2,1)S(1)} collective-permute-done((bf16[48,1024]{1,0:T(8,128)(2,1)S(1)}, bf16[48,1024]{1,0:T(8,128)(2,1)S(1)}, u32[]{:S(2)}, u32[]{:S(2)}) %collective-permute-start.2) | collective-permute-done | bytes 98336 | tf_op jit(solution)/shard_map/ppermute | solution.py:254
  265.3 1.1 add_convert_fusion
  266.3 4.5 %fusion.1.refs_0_ = bf16[8,8,2048]{2,1,0:T(8,128)(2,1)} fusion(bf16[2048,1024]{1,0:T(8,128)(2,1)} %all-gather.2.cloned.1.call-done, bf16[48,1024]{1,0:T(8,128)(2,1)S(1)} %add_convert_fusion, s32[64]{0:T(128)S(1)} %add.46, pred[64]{0:T(512)(128)(4,1)S(1)} %lt.18), kind=kOutput, calls=%fused_computation.5 | convolution fusion | flops 274929664 | bytes 4555072 | tf_op jit(solution)/shard_map/dot_general | solution.py:28
  270.8 8.3 %exchange_9.1 = bf16[8,8,2048]{2,1,0:T(8,128)(2,1)} custom-call(bf16[8,8,2048]{2,1,0:T(8,128)(2,1)} %fusion.1.refs_0_), custom_call_target="tpu_custom_call" | custom-call | tf_op jit(solution)/shard_map/exchange_9/pallas_call | solution.py:75
  279.1 1.0 convert_reduce_fusion
  280.3 3.1 %collective-permute-start.1 = (bf16[48,1024]{1,0:T(8,128)(2,1)}, bf16[48,1024]{1,0:T(8,128)(2,1)S(1)}, u32[]{:S(2)}, u32[]{:S(2)}) collective-permute-start(bf16[48,1024]{1,0:T(8,128)(2,1)} %reduce-scatter.5.cloned.1.call-done), channel_id=1, source_target_pairs={{0,0},{1,1},{2,8},{3,9},{4,16},{5,17},{6,24},{7,25},{8,2},{9,3},{1... | collective-permute-start | bytes 294920 | tf_op jit(solution)/shard_map/ppermute | solution.py:254
  283.4 1.2 fusion
  284.5 7.8 %collective-permute-done.1 = bf16[48,1024]{1,0:T(8,128)(2,1)S(1)} collective-permute-done((bf16[48,1024]{1,0:T(8,128)(2,1)}, bf16[48,1024]{1,0:T(8,128)(2,1)S(1)}, u32[]{:S(2)}, u32[]{:S(2)}) %collective-permute-start.1) | collective-permute-done | bytes 98336 | tf_op jit(solution)/shard_map/ppermute | solution.py:254
  292.4 0.9 fusion.2
  (32 shorter events, 3.8 us)
Async XLA Ops:
  7.2 2.8 copy-start
  7.2 86.5 %all-gather.2.cloned.1.call-start = ((), (), s32[]{:S(2)}) async-start(), calls=%async_computation.2 | async-start | bytes 5242880 | tf_op jit(solution)/shard_map/all_gather | solution.py:260
  7.9 109.9 %reduce-scatter.3.cloned.1.call-start = ((), (), s32[]{:S(2)}) async-start(), calls=%async_computation.3 | async-start | bytes 983040 | tf_op jit(solution)/shard_map/reduce_scatter | solution.py:244
  20.5 28.4 %copy-start.1 = (bf16[8,8,2176]{2,1,0:T(8,128)(2,1)S(1)}, bf16[8,8,2176]{2,1,0:T(8,128)(2,1)}, u32[]{:S(2)}) copy-start(bf16[8,8,2176]{2,1,0:T(8,128)(2,1)} %exchange_0.1) | copy-start | bytes 835588
  56.4 223.9 %reduce-scatter.5.cloned.1.call-start = ((), (), s32[]{:S(2)}) async-start(), calls=%async_computation.4 | async-start | bytes 884736 | tf_op jit(solution)/shard_map/reduce_scatter | solution.py:310
  96.7 22.8 %collective-permute-start = (bf16[48,1024]{1,0:T(8,128)(2,1)S(1)}, bf16[48,1024]{1,0:T(8,128)(2,1)S(1)}, u32[]{:S(2)}, u32[]{:S(2)}) collective-permute-start(bf16[48,1024]{1,0:T(8,128)(2,1)S(1)} %convolution_convert_fusion.7), channel_id=1, source_target_pairs={{0,0},{1,1},{2,8},{3,9},{4,16},{5,17},{6,24},{7,25},{8,2},{9,3},{1... | collective-permute-start | bytes 294920 | tf_op jit(solution)/shard_map/ppermute | solution.py:254
  119.5 0.6 copy-start.2
  236.8 43.3 %copy-start.3 = (f32[2048]{0:T(1024)S(1)}, f32[2048]{0:T(1024)}, u32[]{:S(2)}) copy-start(f32[2048]{0:T(1024)} %param.10) | copy-start | bytes 24580
  236.9 46.5 %copy-start.4 = (s32[1,128]{1,0:T(1,128)S(1)}, s32[1,128]{1,0:T(1,128)}, u32[]{:S(2)}) copy-start(s32[1,128]{1,0:T(1,128)} %param.9) | copy-start | bytes 1540
  251.9 13.3 %collective-permute-start.2 = (bf16[48,1024]{1,0:T(8,128)(2,1)S(1)}, bf16[48,1024]{1,0:T(8,128)(2,1)S(1)}, u32[]{:S(2)}, u32[]{:S(2)}) collective-permute-start(bf16[48,1024]{1,0:T(8,128)(2,1)S(1)} %reduce_sum.40), channel_id=1, source_target_pairs={{0,0},{1,1},{2,8},{3,9},{4,16},{5,17},{6,24},{7,25},{8,2},{9,3},{1... | collective-permute-start | bytes 294920 | tf_op jit(solution)/shard_map/ppermute | solution.py:254
  280.3 12.1 %collective-permute-start.1 = (bf16[48,1024]{1,0:T(8,128)(2,1)}, bf16[48,1024]{1,0:T(8,128)(2,1)S(1)}, u32[]{:S(2)}, u32[]{:S(2)}) collective-permute-start(bf16[48,1024]{1,0:T(8,128)(2,1)} %reduce-scatter.5.cloned.1.call-done), channel_id=1, source_target_pairs={{0,0},{1,1},{2,8},{3,9},{4,16},{5,17},{6,24},{7,25},{8,2},{9,3},{1... | collective-permute-start | bytes 294920 | tf_op jit(solution)/shard_map/ppermute | solution.py:254
Sparse Core Ops, SparseCore 0:
  9.6 84.0 all-gather.1
  96.0 21.7 reduce-scatter.2
  237.0 40.8 reduce-scatter.4
